TPU v7x, 512 devices: a whole 4x8x8 slice. The times are simulated.
512 devices in a mesh: dom: 64 (over z_lo, y, core), col: 8 (over x, z_hi).
Axes of the slice: x: 4, y: 8, z: 8 (z_hi: 2, z_lo: 4; z = z_hi * 4 + z_lo), core: 2. Of those that a mesh axis runs over, the one named last changes fastest.
Arguments:
- features: bfloat16 [128, 16384], P('col', 'dom'), may hold values from -6 to 6
- cached_embed: bfloat16 [128, 16384], P('col'), may hold values from -6 to 6
- staleness: int32 [64], replicated, may hold values from 0 to 15, as said below
- node_counts: int32 [64], replicated, may hold values from 64 to 256, as said below
- neighbours: int32 [16, 16384], P(None, 'dom'), may hold values from 0 to 16383, as said below
- degrees: int32 [16384], P('dom'), may hold values from 1 to 16
- w_self: bfloat16 [128, 256], P('col'), may hold values from -0.5 to 0.5
- w_nbr: bfloat16 [128, 256], P('col'), may hold values from -0.5 to 0.5
- sage_bias: float32 [256], P('col'), may hold values from -3 to 3
- cotangent: bfloat16 [256, 16384], P('col', 'dom'), may hold values from -6 to 6
Outputs:
- activation: bfloat16 [256, 16384], P('col', 'dom')
- grad_feat: bfloat16 [128, 16384], P('col', 'dom')
- grad_self: float32 [128, 256], P('col')
- grad_nbr: float32 [128, 256], P('col')
- grad_bias: float32 [256], P('col')
Inputs may be any that keep to these rules, and one draw needn't show every extreme that they name: Exactly 16 partitions have staleness of 8 or more. `node_counts`: some partition has all 256 node slots live. `neighbours`: every neighbour slot names a live node slot; about half lie in the node's own partition.
All inputs are finite; a program needn't handle non-finite values.
Results may differ from a plain program's by a relative error of at most 0.015.
Values may be sent and summed in bfloat16 or wider, within the bound.
A program may use at most 64 MiB of HBM per device.

v0:
```python
import jax
import jax.numpy as jnp
from jax import lax
from jax.sharding import PartitionSpec as P

LIMIT = 8


def left_product(weight, data):
    return lax.dot_general(
        weight, data, (((0,), (0,)), ((), ())), preferred_element_type=jnp.float32
    )


def right_product(data, grads):
    return lax.dot_general(
        data, grads, (((1,), (1,)), ((), ())), preferred_element_type=jnp.float32
    )


def per_device(
    features,
    cached_embed,
    staleness,
    node_counts,
    neighbours,
    degrees,
    w_self,
    w_nbr,
    sage_bias,
    cotangent,
):
    col_width = features.shape[0]
    part_rows = features.shape[1]
    slot_count = neighbours.shape[0]
    my_index = lax.axis_index("dom")
    fresh_flag = (staleness >= LIMIT).astype(jnp.int32)
    my_fresh = fresh_flag[my_index]
    own_cache = lax.dynamic_slice_in_dim(cached_embed, my_index * part_rows, part_rows, 1)
    own_source = jnp.where(my_fresh == 1, features, own_cache)
    sources = lax.all_gather(own_source, "dom", axis=1, tiled=True)
    local_slot = jnp.arange(part_rows, dtype=jnp.int32)
    live_rows = (local_slot < node_counts[my_index]).astype(jnp.float32)
    slot_index = jnp.arange(slot_count, dtype=jnp.int32)
    used = (slot_index[:, None] < degrees[None, :]).astype(jnp.float32)
    weights = used * (live_rows / degrees.astype(jnp.float32))[None, :]
    gathered = sources[:, neighbours].astype(jnp.float32)
    aggregated = jnp.sum(weights[None, :, :] * gathered, axis=1).astype(jnp.bfloat16)
    partial_pre = left_product(w_self, features) + left_product(w_nbr, aggregated)
    pre_act = (
        lax.psum_scatter(
            partial_pre.astype(jnp.bfloat16), "col", scatter_dimension=0, tiled=True
        ).astype(jnp.float32)
        + sage_bias[:, None]
    )
    sigmoid = 1.0 / (1.0 + jnp.exp(-pre_act))
    activation = (live_rows[None, :] * pre_act * sigmoid).astype(jnp.bfloat16)
    grad_pre = (
        live_rows[None, :]
        * cotangent.astype(jnp.float32)
        * sigmoid
        * (1.0 + pre_act * (1.0 - sigmoid))
    ).astype(jnp.bfloat16)
    grad_full = lax.all_gather(grad_pre, "col", axis=0, tiled=True)
    self_part = right_product(features, grad_full)
    nbr_part = right_product(aggregated, grad_full)
    bias_part = jnp.sum(grad_pre.astype(jnp.float32), axis=1)
    grad_self, grad_nbr, grad_bias = lax.psum((self_part, nbr_part, bias_part), "dom")
    grad_agg = jnp.dot(w_nbr, grad_full, preferred_element_type=jnp.float32).astype(jnp.bfloat16)
    own_term = jnp.dot(w_self, grad_full, preferred_element_type=jnp.float32)
    spread = weights[None, :, :] * grad_agg.astype(jnp.float32)[:, None, :]
    total_rows = cached_embed.shape[1]
    contrib = (
        jnp.zeros((col_width, total_rows), jnp.float32)
        .at[:, neighbours.reshape(-1)]
        .add(spread.reshape(col_width, -1))
    )
    back = lax.psum_scatter(contrib, "dom", scatter_dimension=1, tiled=True)
    grad_feat = (own_term + my_fresh.astype(jnp.float32) * back).astype(jnp.bfloat16)
    return (activation, grad_feat, grad_self, grad_nbr, grad_bias)


def solution(mesh):
    placed = (
        P("col", "dom"),
        P("col", None),
        P(),
        P(),
        P(None, "dom"),
        P("dom"),
        P("col", None),
        P("col", None),
        P("col"),
        P("col", "dom"),
    )
    return jax.shard_map(
        per_device,
        mesh=mesh,
        in_specs=placed,
        out_specs=(P("col", "dom"), P("col", "dom"), P("col", None), P("col", None), P("col")),
        check_vma=False,
    )
```

profile of v0, /device:TPU:2, one launch (start us, length us, event | category | flops | bytes accessed | tf_op | source)
XLA Modules:
  0.0 577.7 jit_solution(13687929819668123944)
XLA Ops:
  7.2 0.0 copy-start
  7.2 0.0 reduce-scatter.3.cloned.1.call-start
  7.2 0.7 compare_convert_fusion
  7.9 1.2 dynamic_slice.9
  9.2 0.6 dynamic_slice.10
  9.8 0.7 fusion.12
  10.5 1.3 convert_divide_fusion
  11.8 0.7 fusion.14
  12.5 0.0 copy-done
  12.5 0.1 copy.21
  12.7 0.8 copy.16
  14.1 99.0 %all_gather.6 = bf16[16,16384]{0,1:T(8,128)(2,1)} all-gather(bf16[16,256]{0,1:T(8,128)(2,1)S(1)} %broadcast_select_fusion), channel_id=1, replica_groups=mesh['dom'=64,'col'=8] {'dom'}, dimensions={1}, use_global_device_ids=true | all-gather | bytes 532480 | tf_op jit(solution)/shard_map/all_gather | solution.py:41
  113.2 0.0 copy-start.4
  113.2 0.0 copy-start.1
  113.2 0.0 copy-start.3
  113.2 0.0 copy-start.2
  113.2 0.0 copy-start.5
  113.2 0.0 copy-start.6
  113.2 13.8 %gather_fusion = bf16[4096,16]{1,0:T(8,128)(2,1)S(1)} fusion(bf16[16,16384]{0,1:T(8,128)(2,1)} %all_gather.6, s32[4096]{0:T(1024)S(1)} %broadcast_clamp_fusion), kind=kCustom, calls=%fused_computation | custom fusion | bytes 278528 | tf_op jit(solution)/shard_map/gather | solution.py:47
  127.0 0.7 fusion.2
  127.7 0.0 copy-done.4
  127.7 0.2 convolution_bitcast_fusion
  128.0 0.0 copy-done.1
  128.0 0.0 copy-done.3
  128.0 0.9 fusion.4
  128.9 0.0 reduce-scatter.3.cloned.1.call-update
  128.9 0.0 reduce-scatter.5.cloned.1.call-start
  128.9 0.0 copy-done.2
  129.0 0.7 compare_convert_fusion.1
  129.7 84.0 %reduce-scatter.3.cloned.1.call-done = bf16[32,256]{1,0:T(8,128)(2,1)} async-done(((bf16[256,256]{1,0:T(8,128)(2,1)}), bf16[32,256]{1,0:T(8,128)(2,1)}) %reduce-scatter.3.cloned.1.call-update) | async-done | bytes 16400 | tf_op jit(solution)/shard_map/reduce_scatter | solution.py:51
  213.6 0.0 copy-done.5
  213.6 0.0 copy-done.6
  213.6 1.5 convert_reduce_fusion
  215.2 42.2 %all_gather.7 = bf16[256,256]{1,0:T(8,128)(2,1)S(1)} all-gather(bf16[32,256]{1,0:T(8,128)(2,1)S(1)} %get-tuple-element.9), channel_id=1, replica_groups=mesh['dom'=64,'col'=8] {'col'}, dimensions={0}, use_global_device_ids=true | all-gather | bytes 147456 | tf_op jit(solution)/shard_map/all_gather | solution.py:64
  257.3 0.1 fusion.8
  257.5 0.1 copy.18
  257.6 0.6 bitcast_multiply_fusion
  258.2 26.1 %scatter_custom_fusion = f32[16,16384]{0,1:T(8,128)} fusion(s32[4096]{0:T(1024)S(1)} %bitcast.50, f32[]{:T(128)} %constant.14.clone.1, f32[16,4096]{0,1:T(8,128)S(1)} %bitcast_multiply_fusion), kind=kCustom, calls=%fused_computation.2 | custom fusion | flops 65536 | bytes 3145732 | tf_op jit(solution)/shard_map/scatter-add | solution.py:76
  284.3 6.0 %copy.19 = f32[16,16384]{1,0:T(8,128)} copy(f32[16,16384]{0,1:T(8,128)} %scatter_custom_fusion) | data formatting | bytes 2097152 | tf_op jit(solution)/shard_map/scatter-add | solution.py:76
  290.3 0.0 reduce-scatter.5.cloned.1.call-update
  291.0 0.1 convolution_bitcast_fusion.2
  291.1 0.2 fusion.15
  291.3 265.0 %all-reduce = (f32[16,256]{1,0:T(8,128)}, f32[16,256]{1,0:T(8,128)}, f32[32]{0:T(128)}) all-reduce(f32[16,256]{1,0:T(8,128)S(1)} %convolution_bitcast_fusion.2, f32[16,256]{1,0:T(8,128)S(1)} %fusion.15, f32[32]{0:T(128)S(1)} %get-tuple-element.8), channel_id=1, replica_groups=mesh['dom'=64,'col'=8] {'dom'}, use_global_device_ids=true, to_apply=%region_4.5 | all-reduce | flops 8224 | bytes 65792 | tf_op jit(solution)/shard_map/psum | solution.py:68
  556.3 13.1 %reduce-scatter.5.cloned.1.call-done = f32[16,256]{1,0:T(8,128)} async-done(((f32[16,16384]{1,0:T(8,128)}), f32[16,256]{1,0:T(8,128)}) %reduce-scatter.5.cloned.1.call-update) | async-done | bytes 16400 | tf_op jit(solution)/shard_map/reduce_scatter | solution.py:78
  569.4 1.5 fusion.6
  (7 shorter events, 0.1 us)
Async XLA Ops:
  7.2 5.4 copy-start
  7.2 206.4 %reduce-scatter.3.cloned.1.call-start = ((), (), s32[]{:S(2)}) async-start(), calls=%async_computation.2 | async-start | bytes 147456 | tf_op jit(solution)/shard_map/reduce_scatter | solution.py:51
  113.2 14.6 %copy-start.4 = (bf16[16,256]{1,0:T(8,128)(2,1)S(1)}, bf16[16,256]{1,0:T(8,128)(2,1)}, u32[]{:S(2)}) copy-start(bf16[16,256]{1,0:T(8,128)(2,1)} %param.17) | copy-start | bytes 24580
  113.2 14.8 %copy-start.1 = (bf16[16,256]{1,0:T(8,128)(2,1)S(1)}, bf16[16,256]{1,0:T(8,128)(2,1)}, u32[]{:S(2)}) copy-start(bf16[16,256]{1,0:T(8,128)(2,1)} %param.10) | copy-start | bytes 24580
  113.2 14.8 %copy-start.3 = (bf16[16,256]{1,0:T(8,128)(2,1)S(1)}, bf16[16,256]{1,0:T(8,128)(2,1)}, u32[]{:S(2)}) copy-start(bf16[16,256]{1,0:T(8,128)(2,1)} %param.16) | copy-start | bytes 24580
  113.2 15.8 %copy-start.2 = (s32[16,256]{1,0:T(8,128)S(1)}, s32[16,256]{1,0:T(8,128)}, u32[]{:S(2)}) copy-start(s32[16,256]{1,0:T(8,128)} %param.14) | copy-start | bytes 49156
  113.2 100.5 %copy-start.5 = (bf16[32,256]{1,0:T(8,128)(2,1)S(1)}, bf16[32,256]{1,0:T(8,128)(2,1)}, u32[]{:S(2)}) copy-start(bf16[32,256]{1,0:T(8,128)(2,1)} %param.19) | copy-start | bytes 49156
  113.2 100.5 %copy-start.6 = (f32[32]{0:T(128)S(1)}, f32[32]{0:T(128)}, u32[]{:S(2)}) copy-start(f32[32]{0:T(128)} %param.18) | copy-start | bytes 388
  128.9 440.5 %reduce-scatter.5.cloned.1.call-start = ((), (), s32[]{:S(2)}) async-start(), calls=%async_computation.3 | async-start | bytes 1064960 | tf_op jit(solution)/shard_map/reduce_scatter | solution.py:78
Sparse Core Ops, SparseCore 0:
  129.0 84.5 reduce-scatter.2
  290.4 278.9 reduce-scatter.4
where the time goes:
time: 578 us
  blocking collectives  406 us (70%)
  waiting for transfers between devices  97.1 us (17%)
  other arithmetic  33.1 us (6%)
  local copies, waits for them, and re-layouts  22.8 us (4%)
  between operations  15.5 us (3%)
    psum x1, blocking collectives, per_device(): lax.psum((self_part, nbr_part, bias_part), 'dom')  265 us
    all_gather x1, blocking collectives, per_device(): sources = lax.all_gather(own_source, 'dom', axis=1, tiled=True)  99 us
    reduce_scatter x1, waiting for transfers between devices, per_device(): lax.psum_scatter(partial_pre.astype(jnp.bfloat16), 'col', scatter_dimensi...  84 us
    all_gather x1, blocking collectives, per_device(): grad_full = lax.all_gather(grad_pre, 'col', axis=0, tiled=True)  42.2 us
    scatter-add x1, other arithmetic, per_device(): contrib = jnp.zeros((col_width, total_rows), jnp.float32).at[:, neighbour...  26.1 us
    gather x1, local copies, waits for them, and re-layouts, per_device(): gathered = sources[:, neighbours].astype(jnp.float32)  13.8 us
    reduce_scatter x1, waiting for transfers between devices, per_device(): back = lax.psum_scatter(contrib, 'dom', scatter_dimension=1, tiled=True)  13.1 us
  transfers between devices with their start and end apart: 2, of which 2 were waited for; matrix products, arithmetic and copies ran while one was open for 0% of the time, Pallas kernels for 0%

commit v1 on v0

--- a/solution.py
+++ b/solution.py
@@ -30,6 +30,14 @@
     sage_bias,
     cotangent,
 ):
+
+    def goods_track(q_in, where_dim):
+        out_arr = jax.lax.axis_size("dom")
+        carry_in = jnp.stack(out_arr * [q_in], axis=0)
+        even = jax.lax.all_to_all(carry_in, "dom", 0, 0)
+        z = jnp.concatenate(even, axis=where_dim)
+        return z
+
     col_width = features.shape[0]
     part_rows = features.shape[1]
     slot_count = neighbours.shape[0]
@@ -38,7 +46,7 @@
     my_fresh = fresh_flag[my_index]
     own_cache = lax.dynamic_slice_in_dim(cached_embed, my_index * part_rows, part_rows, 1)
     own_source = jnp.where(my_fresh == 1, features, own_cache)
-    sources = lax.all_gather(own_source, "dom", axis=1, tiled=True)
+    sources = goods_track(own_source, 1)
     local_slot = jnp.arange(part_rows, dtype=jnp.int32)
     live_rows = (local_slot < node_counts[my_index]).astype(jnp.float32)
     slot_index = jnp.arange(slot_count, dtype=jnp.int32)

time: 578 us -> 513 us (0.89)
  the two profiles are of different devices: /device:TPU:2 before, /device:TPU:4 now
where the time goes in v1:
time: 513 us; the launch traced here: 512 us
  blocking collectives  307 us (60%)
  waiting for transfers between devices  113 us (22%)
  other arithmetic  33.7 us (7%)
  local copies, waits for them, and re-layouts  26.4 us (5%)
  between operations  15.5 us (3%)
  starting transfers between devices  13.6 us (3%)
    psum x1, blocking collectives, per_device(): lax.psum((self_part, nbr_part, bias_part), 'dom')  265 us
    reduce_scatter x1, waiting for transfers between devices, per_device(): lax.psum_scatter(partial_pre.astype(jnp.bfloat16), 'col', scatter_dimensi...  85.2 us
    all_gather x1, blocking collectives, per_device(): grad_full = lax.all_gather(grad_pre, 'col', axis=0, tiled=True)  41.9 us
    scatter-add x1, other arithmetic, per_device(): contrib = jnp.zeros((col_width, total_rows), jnp.float32).at[:, neighbour...  26.1 us
    reduce_scatter x1, waiting for transfers between devices, per_device(): back = lax.psum_scatter(contrib, 'dom', scatter_dimension=1, tiled=True)  14.5 us
    gather x1, local copies, waits for them, and re-layouts, per_device(): gathered = sources[:, neighbours].astype(jnp.float32)  13.8 us
    all_to_all x1, starting transfers between devices, goods_track(): even = jax.lax.all_to_all(carry_in, 'dom', 0, 0)  13.5 us
    all_to_all x1, waiting for transfers between devices, goods_track(): even = jax.lax.all_to_all(carry_in, 'dom', 0, 0)  13 us
  transfers between devices with their start and end apart: 3, of which 3 were waited for; matrix products, arithmetic and copies ran while one was open for 1% of the time, Pallas kernels for 0%

profile of v1, /device:TPU:4, one launch (start us, length us, event | category | flops | bytes accessed | tf_op | source)
XLA Modules:
  0.0 512.0 jit_solution(12307607096361422659)
XLA Ops:
  7.2 0.0 copy-start
  7.2 0.7 compare_convert_fusion
  7.8 0.6 dynamic_slice.10
  9.1 0.7 dynamic-slice_select_fusion
  9.8 0.8 stack.2
  10.6 13.5 %all-to-all-start = ((bf16[64,16,256]{2,1,0:T(8,128)(2,1)}), bf16[64,16,256]{2,1,0:T(8,128)(2,1)S(1)}, u32[]{:S(2)}, u32[]{:S(2)}) async-start(bf16[64,16,256]{2,1,0:T(8,128)(2,1)} %stack.2), calls=%async_computation | async-start | bytes 1048576 | tf_op jit(solution)/shard_map/all_to_all | solution.py:37
  24.2 0.0 reduce-scatter.3.cloned.1.call-start
  24.2 1.2 dynamic_slice.9
  25.5 0.7 copy.25
  26.2 0.7 fusion.12
  26.9 1.3 convert_divide_fusion
  28.3 0.7 fusion.14
  29.0 13.0 %all-to-all-done = bf16[64,16,256]{2,1,0:T(8,128)(2,1)S(1)} async-done(((bf16[64,16,256]{2,1,0:T(8,128)(2,1)}), bf16[64,16,256]{2,1,0:T(8,128)(2,1)S(1)}, u32[]{:S(2)}, u32[]{:S(2)}) %all-to-all-start) | async-done | bytes 524320 | tf_op jit(solution)/shard_map/all_to_all | solution.py:37
  42.0 3.1 copy.19
  45.1 0.0 copy-start.1
  45.1 0.0 copy-start.2
  45.1 0.0 copy-start.3
  45.1 0.0 copy-start.4
  45.1 13.8 %gather_fusion = bf16[4096,16]{1,0:T(8,128)(2,1)S(1)} fusion(bf16[16,16384]{0,1:T(8,128)(2,1)} %bitcast.47, s32[4096]{0:T(1024)S(1)} %broadcast_clamp_fusion), kind=kCustom, calls=%fused_computation | custom fusion | bytes 278528 | tf_op jit(solution)/shard_map/gather | solution.py:55
  58.9 0.7 fusion.2
  59.6 0.0 copy-done
  59.6 0.2 convolution_bitcast_fusion
  59.8 0.0 copy-done.1
  59.9 0.0 copy-done.2
  59.9 0.9 fusion.4
  60.7 0.0 reduce-scatter.3.cloned.1.call-update
  60.8 0.0 reduce-scatter.5.cloned.1.call-start
  60.9 0.7 compare_convert_fusion.1
  61.5 85.2 %reduce-scatter.3.cloned.1.call-done = bf16[32,256]{1,0:T(8,128)(2,1)} async-done(((bf16[256,256]{1,0:T(8,128)(2,1)}), bf16[32,256]{1,0:T(8,128)(2,1)}) %reduce-scatter.3.cloned.1.call-update) | async-done | bytes 16400 | tf_op jit(solution)/shard_map/reduce_scatter | solution.py:59
  146.7 0.0 copy-done.3
  146.7 0.0 copy-done.4
  146.7 1.5 convert_reduce_fusion
  148.3 41.9 %all_gather.3 = bf16[256,256]{1,0:T(8,128)(2,1)S(1)} all-gather(bf16[32,256]{1,0:T(8,128)(2,1)S(1)} %get-tuple-element.9), channel_id=1, replica_groups=mesh['dom'=64,'col'=8] {'col'}, dimensions={0}, use_global_device_ids=true | all-gather | bytes 147456 | tf_op jit(solution)/shard_map/all_gather | solution.py:72
  190.2 0.1 fusion.8
  190.3 0.1 copy.21
  190.4 0.6 bitcast_multiply_fusion
  191.1 26.1 %scatter_custom_fusion = f32[16,16384]{0,1:T(8,128)} fusion(s32[4096]{0:T(1024)S(1)} %bitcast.54, f32[]{:T(128)} %constant.14.clone.1, f32[16,4096]{0,1:T(8,128)S(1)} %bitcast_multiply_fusion), kind=kCustom, calls=%fused_computation.2 | custom fusion | flops 65536 | bytes 3145732 | tf_op jit(solution)/shard_map/scatter-add | solution.py:84
  217.2 6.0 %copy.22 = f32[16,16384]{1,0:T(8,128)} copy(f32[16,16384]{0,1:T(8,128)} %scatter_custom_fusion) | data formatting | bytes 2097152 | tf_op jit(solution)/shard_map/scatter-add | solution.py:84
  223.2 0.0 reduce-scatter.5.cloned.1.call-update
  223.8 0.1 convolution_bitcast_fusion.2
  224.0 0.2 fusion.15
  224.2 265.0 %all-reduce = (f32[16,256]{1,0:T(8,128)}, f32[16,256]{1,0:T(8,128)}, f32[32]{0:T(128)}) all-reduce(f32[16,256]{1,0:T(8,128)S(1)} %convolution_bitcast_fusion.2, f32[16,256]{1,0:T(8,128)S(1)} %fusion.15, f32[32]{0:T(128)S(1)} %get-tuple-element.8), channel_id=1, replica_groups=mesh['dom'=64,'col'=8] {'dom'}, use_global_device_ids=true, to_apply=%region_4.5 | all-reduce | flops 8224 | bytes 65792 | tf_op jit(solution)/shard_map/psum | solution.py:76
  489.1 14.5 %reduce-scatter.5.cloned.1.call-done = f32[16,256]{1,0:T(8,128)} async-done(((f32[16,16384]{1,0:T(8,128)}), f32[16,256]{1,0:T(8,128)}) %reduce-scatter.5.cloned.1.call-update) | async-done | bytes 16400 | tf_op jit(solution)/shard_map/reduce_scatter | solution.py:86
  503.7 1.5 fusion.6
  (4 shorter events, 0.0 us)
Async XLA Ops:
  7.2 52.4 %copy-start = (bf16[16,256]{1,0:T(8,128)(2,1)S(1)}, bf16[16,256]{1,0:T(8,128)(2,1)}, u32[]{:S(2)}) copy-start(bf16[16,256]{1,0:T(8,128)(2,1)} %param.17) | copy-start | bytes 24580
  10.6 31.3 %all-to-all-start = ((bf16[64,16,256]{2,1,0:T(8,128)(2,1)}), bf16[64,16,256]{2,1,0:T(8,128)(2,1)S(1)}, u32[]{:S(2)}, u32[]{:S(2)}) async-start(bf16[64,16,256]{2,1,0:T(8,128)(2,1)} %stack.2), calls=%async_computation | async-start | bytes 1048576 | tf_op jit(solution)/shard_map/all_to_all | solution.py:37
  24.2 122.5 %reduce-scatter.3.cloned.1.call-start = ((), (), s32[]{:S(2)}) async-start(), calls=%async_computation.3 | async-start | bytes 147456 | tf_op jit(solution)/shard_map/reduce_scatter | solution.py:59
  45.1 14.8 %copy-start.1 = (bf16[16,256]{1,0:T(8,128)(2,1)S(1)}, bf16[16,256]{1,0:T(8,128)(2,1)}, u32[]{:S(2)}) copy-start(bf16[16,256]{1,0:T(8,128)(2,1)} %param.10) | copy-start | bytes 24580
  45.1 14.8 %copy-start.2 = (bf16[16,256]{1,0:T(8,128)(2,1)S(1)}, bf16[16,256]{1,0:T(8,128)(2,1)}, u32[]{:S(2)}) copy-start(bf16[16,256]{1,0:T(8,128)(2,1)} %param.16) | copy-start | bytes 24580
  45.1 101.7 %copy-start.3 = (bf16[32,256]{1,0:T(8,128)(2,1)S(1)}, bf16[32,256]{1,0:T(8,128)(2,1)}, u32[]{:S(2)}) copy-start(bf16[32,256]{1,0:T(8,128)(2,1)} %param.19) | copy-start | bytes 49156
  45.1 101.7 %copy-start.4 = (f32[32]{0:T(128)S(1)}, f32[32]{0:T(128)}, u32[]{:S(2)}) copy-start(f32[32]{0:T(128)} %param.18) | copy-start | bytes 388
  60.8 442.9 %reduce-scatter.5.cloned.1.call-start = ((), (), s32[]{:S(2)}) async-start(), calls=%async_computation.4 | async-start | bytes 1064960 | tf_op jit(solution)/shard_map/reduce_scatter | solution.py:86
Sparse Core Ops, SparseCore 0:
  60.9 85.8 reduce-scatter.2
  223.3 280.3 reduce-scatter.4
